TPU v7x, 256 devices: a whole 4x4x8 slice. The times are simulated.
256 devices in a mesh: ctx: 32 (over y, x, core), head: 4 (over z_lo), dp: 2 (over z_hi).
Axes of the slice: x: 4, y: 4, z: 8 (z_hi: 2, z_lo: 4; z = z_hi * 4 + z_lo), core: 2. Of those that a mesh axis runs over, the one named last changes fastest.
Arguments:
- queries: bfloat16 [2, 8192, 4096], P('dp', 'ctx', 'head'), may hold values from -6 to 6
- keys: bfloat16 [2, 8192, 4096], P('dp', 'ctx', 'head'), may hold values from -6 to 6
- values: bfloat16 [2, 8192, 4096], P('dp', 'ctx', 'head'), may hold values from -6 to 6
- log_decay: float32 [2, 32, 8192], P('dp', 'head', 'ctx'), may hold values from -1.5 to 0
- w_out: bfloat16 [128, 32, 3072], P(('ctx', 'dp'), 'head'), may hold values from -0.09375 to 0.09375
- grad_out: bfloat16 [2, 8192, 3072], P('dp', 'ctx'), may hold values from -6 to 6
Outputs:
- mixed: bfloat16 [2, 8192, 3072], P('dp', 'ctx', 'head')
- query_grad: bfloat16 [2, 8192, 4096], P('dp', 'ctx', 'head')
- key_grad: bfloat16 [2, 8192, 4096], P('dp', 'ctx', 'head')
- value_grad: bfloat16 [2, 8192, 4096], P('dp', 'ctx', 'head')
- w_grad: float32 [128, 32, 3072], P(('ctx', 'dp'), 'head')
All inputs are finite; a program needn't handle non-finite values.
Results may differ from a plain program's by a relative error of at most 0.015.
Values may be sent and summed in bfloat16 or wider, within the bound.
A program may use at most 128 MiB of HBM per device.

v0:
```python
import jax
import jax.numpy as jnp
from jax import lax
from jax.sharding import PartitionSpec as P

DH = 128
BLOCK = 256


def entering_2(array, axis, combine, identity, reverse):
    devices, mine = (lax.axis_size(axis), lax.axis_index(axis))
    everything = jax.tree.map(lambda part: lax.all_gather(part, axis), array)
    start = jax.tree.map(
        lambda part, zero: jnp.broadcast_to(jnp.asarray(zero, part.dtype), part.shape),
        array,
        identity,
    )

    def lap(k, before):
        at = devices - 1 - k if reverse else k
        reached = at > mine if reverse else at < mine
        new = combine(before, jax.tree.map(lambda part: part[at], everything))
        return jax.tree.map(lambda a, b: jnp.where(reached, a, b), new, before)

    return lax.fori_loop(0, devices, lap, start)


def block_weights(cumul):
    width = cumul.shape[-1]
    places = jnp.arange(width)
    lower = places[:, None] >= places[None, :]
    spread = cumul[..., :, None] - cumul[..., None, :]
    return jnp.exp(jnp.where(lower, spread, -jnp.inf))


def forward_join(earlier, later):
    return (earlier[0] * later[0], later[0][:, None, None] * earlier[1] + later[1])


def backward_combine(earlier, later):
    return (earlier[0] * later[0], later[1] + later[0][:, None, None] * earlier[1])


def shards(queries, keys, values, log_decay, w_out, grad_out):
    groups = log_decay.shape[1]
    length_here = queries.shape[1]
    tile_number = length_here // BLOCK
    scale = 1.0 / DH
    query_blocks = queries[0].reshape(tile_number, BLOCK, groups, DH)
    key_blocks = keys[0].reshape(tile_number, BLOCK, groups, DH)
    value_blocks = values[0].reshape(tile_number, BLOCK, groups, DH)
    places = jnp.arange(BLOCK)
    upper = (places[:, None] <= places[None, :]).astype(jnp.float32)
    cumul = jnp.einsum(
        "hnj,jt->hnt",
        log_decay[0].reshape(groups, tile_number, BLOCK),
        upper,
        precision=lax.Precision.HIGHEST,
    )
    weights = block_weights(cumul)
    decay_multiplier = jnp.transpose(scale * jnp.exp(cumul), (1, 2, 0))[..., None]
    tail = jnp.transpose(jnp.exp(cumul[..., -1:] - cumul), (1, 2, 0))[..., None]
    block_decay = jnp.exp(cumul[..., -1])
    ones_decay = jnp.ones((groups,), jnp.float32)
    zero_state = jnp.zeros((groups, DH, DH), jnp.float32)
    scores = jnp.einsum(
        "nthd,njhd->hntj", query_blocks, key_blocks, preferred_element_type=jnp.float32
    )
    probs = (scores * scale * weights).astype(jnp.bfloat16)
    intra = jnp.einsum("hntj,njhd->nthd", probs, value_blocks, preferred_element_type=jnp.float32)
    keys_weighted = (key_blocks * tail).astype(jnp.bfloat16)
    contrib = jnp.einsum(
        "nthd,nthe->hnde", keys_weighted, value_blocks, preferred_element_type=jnp.float32
    )
    total_decay = ones_decay
    total_state = zero_state
    index = 0
    total_state = block_decay[:, index][:, None, None] * total_state + contrib[:, index]
    total_decay = total_decay * block_decay[:, index]
    incoming = entering_2(
        (total_decay, total_state), "ctx", forward_join, (ones_decay, zero_state), False
    )[1]
    running = incoming
    index = 0
    entering = [running]
    state_low = jnp.stack(entering, axis=1).astype(jnp.bfloat16)
    inter = jnp.einsum(
        "nthd,hnde->nthe", query_blocks, state_low, preferred_element_type=jnp.float32
    )
    attended = (intra + inter * decay_multiplier).astype(jnp.bfloat16)
    attended_row_list = attended.reshape(length_here, groups, DH)
    panel = lax.all_gather(w_out, ("ctx", "dp"), axis=0, tiled=True)
    partial_out = jnp.einsum(
        "thd,dho->to", attended_row_list, panel, preferred_element_type=jnp.float32
    )
    mixed = lax.psum_scatter(
        partial_out.astype(jnp.bfloat16), "head", scatter_dimension=1, tiled=True
    )
    cotangent = grad_out[0]
    grad_heads = jnp.einsum(
        "to,dho->thd", cotangent, panel, preferred_element_type=jnp.float32
    ).astype(jnp.bfloat16)
    grad_blocks = grad_heads.reshape(tile_number, BLOCK, groups, DH)
    w_grad = lax.psum_scatter(
        jnp.einsum("thd,to->dho", attended_row_list, cotangent, preferred_element_type=jnp.float32),
        ("ctx", "dp"),
        scatter_dimension=0,
        tiled=True,
    )
    logit_gradient = jnp.einsum(
        "nthe,njhe->hntj", grad_blocks, value_blocks, preferred_element_type=jnp.float32
    )
    dprobs = (logit_gradient * scale * weights).astype(jnp.bfloat16)
    queries_weighted = (query_blocks * decay_multiplier).astype(jnp.bfloat16)
    local_grad = jnp.einsum(
        "nthd,nthe->hnde", queries_weighted, grad_blocks, preferred_element_type=jnp.float32
    )
    faded_carry = ones_decay
    after_state = zero_state
    for index in reversed(range(tile_number)):
        after_state = block_decay[:, index][:, None, None] * after_state + local_grad[:, index]
        faded_carry = faded_carry * block_decay[:, index]
    leaving = entering_2(
        (faded_carry, after_state), "ctx", backward_combine, (ones_decay, zero_state), True
    )[1]
    exiting = []
    running = leaving
    for index in reversed(range(tile_number)):
        exiting = [running] + exiting
        running = block_decay[:, index][:, None, None] * running + local_grad[:, index]
    back_low = jnp.stack(exiting, axis=1).astype(jnp.bfloat16)
    query_grad = (
        jnp.einsum("hntj,njhd->nthd", dprobs, key_blocks, preferred_element_type=jnp.float32)
        + jnp.einsum("nthe,hnde->nthd", grad_blocks, state_low, preferred_element_type=jnp.float32)
        * decay_multiplier
    )
    key_grad = jnp.einsum(
        "hntj,nthd->njhd", dprobs, query_blocks, preferred_element_type=jnp.float32
    ) + tail * jnp.einsum(
        "nthe,hnde->nthd", value_blocks, back_low, preferred_element_type=jnp.float32
    )
    value_grad = jnp.einsum(
        "hntj,nthe->njhe", probs, grad_blocks, preferred_element_type=jnp.float32
    ) + tail * jnp.einsum(
        "nthd,hnde->nthe", key_blocks, back_low, preferred_element_type=jnp.float32
    )
    flat = (1, length_here, groups * DH)
    return (
        mixed[None],
        query_grad.astype(jnp.bfloat16).reshape(flat),
        key_grad.astype(jnp.bfloat16).reshape(flat),
        value_grad.astype(jnp.bfloat16).reshape(flat),
        w_grad,
    )


def solution(mesh):
    return jax.shard_map(
        shards,
        mesh=mesh,
        in_specs=(
            P("dp", "ctx", "head"),
            P("dp", "ctx", "head"),
            P("dp", "ctx", "head"),
            P("dp", "head", "ctx"),
            P(("ctx", "dp"), "head", None),
            P("dp", "ctx", None),
        ),
        out_specs=(
            P("dp", "ctx", "head"),
            P("dp", "ctx", "head"),
            P("dp", "ctx", "head"),
            P("dp", "ctx", "head"),
            P(("ctx", "dp"), "head", None),
        ),
        check_vma=False,
    )
```

profile of v0, /device:TPU:1, one launch (start us, length us, event | category | flops | bytes accessed | tf_op | source)
XLA Modules:
  0.0 551.8 jit_solution(11020169705880743914)
XLA Ops:
  9.1 1.3 copy.96
  12.5 1.2 copy.94
  13.7 104.7 %all-gather.7.cloned.1.call-done = bf16[128,8,3072]{2,1,0:T(8,128)(2,1)} async-done(((bf16[2,8,3072]{2,1,0:T(8,128)(2,1)}), bf16[128,8,3072]{2,1,0:T(8,128)(2,1)}) %all-gather.7.cloned.1.call-update) | async-done | bytes 6291472 | tf_op jit(solution)/shard_map/all_gather | solution.py:92
  118.4 4.6 fusion.11
  126.6 63.6 %all-reduce = f32[256]{0:T(256)S(1)} all-reduce(f32[256]{0:T(256)S(1)} %dynamic-update-slice), channel_id=2, replica_groups=mesh['ctx'=32,'head'=4,'dp'=2] {'ctx'}, use_global_device_ids=true, to_apply=%add | all-reduce | flops 256 | bytes 2048
  190.3 1.8 multiply_convert_fusion.1
  193.1 1.4 convolution_bitcast_fusion.8
  194.5 39.3 %while.30 = (s32[]{:T(128)}, f32[8,128,128]{2,1,0:T(8,128)S(1)}, s32[]{:T(128)}, f32[32,8]{1,0:T(8,128)S(1)}, f32[32,8,128,128]{3,2,1,0:T(8,128)}, /*index=5*/s32[]{:T(128)}, s32[]{:T(128)}) while((s32[]{:T(128)}, f32[8,128,128]{2,1,0:T(8,128)S(1)}, s32[]{:T(128)}, f32[32,8]{1,0:T(8,128)S(1)}, f32[32,8,128,128]{3,2,1,0:T(8,128)}, ...), condition=%wide.region_1.2_spmd.clone, body=%wide.region_0.1_spmd.clone.sunk | while | flops 524292 | bytes 1573073 | solution.py:25
  205.5 1.2 fusion.58
  206.7 1.2 fusion.58
  208.0 1.3 fusion.58
  211.7 1.2 fusion.58
  212.9 1.2 fusion.58
  214.2 1.2 fusion.58
  216.6 1.2 fusion.58
  232.5 1.3 fusion.58
  233.8 1.9 fusion.25
  236.5 17.9 %fusion.7 = bf16[256,3072]{1,0:T(8,128)(2,1)} fusion(bf16[256,8,128]{2,0,1:T(8,128)(2,1)S(1)} %fusion.25, bf16[128,8,3072]{2,1,0:T(8,128)(2,1)} %all-gather.7.cloned.1.call-done), kind=kOutput, calls=%fused_computation.10 | convolution fusion | flops 1611399168 | bytes 8388608 | tf_op jit(solution)/shard_map/thd,dho->to/dot_general | solution.py:93
  255.5 6.4 %convolution_bitcast_fusion = f32[128,8,3072]{2,0,1:T(8,128)} fusion(bf16[256,8,128]{2,0,1:T(8,128)(2,1)S(1)} %copy-done.10, bf16[1,256,3072]{2,1,0:T(8,128)(2,1)S(1)} %copy-done), kind=kOutput, calls=%fused_computation.6 | convolution fusion | flops 1610612736 | bytes 14680064 | tf_op jit(solution)/shard_map/thd,to->dho/dot_general | solution.py:105
  261.9 16.7 %copy.81 = f32[128,8,3072]{2,1,0:T(8,128)} copy(f32[128,8,3072]{2,0,1:T(8,128)} %convolution_bitcast_fusion) | data formatting | bytes 25165824 | tf_op jit(solution)/shard_map/thd,to->dho/transpose | solution.py:105
  280.7 1.3 convolution_bitcast_fusion.5
  282.4 1.3 convolution_bitcast_fusion.6
  285.9 39.4 %while.31 = (s32[]{:T(128)}, f32[8,128,128]{2,1,0:T(8,128)S(1)}, s32[]{:T(128)}, f32[32,8,128,128]{3,2,1,0:T(8,128)}, f32[32,8]{1,0:T(8,128)S(1)}, /*index=5*/s32[]{:T(128)}, s32[]{:T(128)}, s32[]{:T(128)}, s32[]{:T(128)}) while((s32[]{:T(128)}, f32[8,128,128]{2,1,0:T(8,128)S(1)}, s32[]{:T(128)}, f32[32,8,128,128]{3,2,1,0:T(8,128)}, ...), condition=%wide.region_4.5_spmd.clone, body=%wide.region_3.4_spmd.clone.sunk | while | flops 524296 | bytes 1573135 | solution.py:25
  285.9 1.3 fusion.59
  293.4 1.2 fusion.59
  295.8 1.2 fusion.59
  304.4 1.2 fusion.59
  308.1 1.2 fusion.59
  314.3 1.2 fusion.59
  326.4 2.2 copy.83
  328.6 1.6 fusion.22
  331.2 214.1 %reduce-scatter.5.cloned.1.call-done = f32[2,8,3072]{2,1,0:T(8,128)} async-done(((f32[128,8,3072]{2,1,0:T(8,128)}), f32[2,8,3072]{2,1,0:T(8,128)}) %reduce-scatter.5.cloned.1.call-update) | async-done | bytes 196624 | tf_op jit(solution)/shard_map/reduce_scatter | solution.py:104
  (184 shorter events, 75.7 us)
Async XLA Ops:
  7.2 111.3 %copy-start = (bf16[1,256,3072]{2,1,0:T(8,128)(2,1)S(1)}, bf16[1,256,3072]{2,1,0:T(8,128)(2,1)}, u32[]{:S(2)}) copy-start(bf16[1,256,3072]{2,1,0:T(8,128)(2,1)} %param.15) | copy-start | bytes 4718596
  7.2 3.6 copy-start.16
  7.2 111.2 %all-gather.7.cloned.1.call-start = ((), (), s32[]{:S(2)}) async-start(), calls=%async_computation.2 | async-start | bytes 6389760 | tf_op jit(solution)/shard_map/all_gather | solution.py:92
  7.9 186.6 %all-gather.9.cloned.1.call-start = ((), (), s32[]{:S(2)}) async-start(), calls=%async_computation.5 | async-start | bytes 17301504 | tf_op jit(solution)/shard_map/all_gather | solution.py:12
  9.1 3.3 copy-start.4
  10.8 1.6 copy-start.14
  12.4 273.4 %all-gather.11.cloned.1.call-start = ((), (), s32[]{:S(2)}) async-start(), calls=%async_computation.6 | async-start | bytes 17301504 | tf_op jit(solution)/shard_map/all_gather | solution.py:12
  13.7 220.1 %copy-start.2 = (bf16[1,256,1024]{1,2,0:T(8,128)(2,1)}, bf16[1,256,1024]{1,2,0:T(8,128)(2,1)S(1)}, u32[]{:S(2)}) copy-start(bf16[1,256,1024]{1,2,0:T(8,128)(2,1)S(1)} %copy.94) | copy-start | bytes 1572868
  123.0 0.8 copy-start.11
  123.0 2.0 copy-start.17
  125.0 206.2 %reduce-scatter.3.cloned.1.call-start = ((), (), s32[]{:S(2)}) async-start(), calls=%async_computation.3 | async-start | bytes 1966080 | tf_op jit(solution)/shard_map/reduce_scatter | solution.py:96
  192.1 1.0 copy-start.6
  235.7 0.8 copy-start.9
  254.4 1.1 copy-start.10
  254.5 290.8 %reduce-scatter.5.cloned.1.call-start = ((), (), s32[]{:S(2)}) async-start(), calls=%async_computation.4 | async-start | bytes 12779520 | tf_op jit(solution)/shard_map/reduce_scatter | solution.py:104
  278.6 1.0 copy-start.12
  279.6 1.0 copy-start.3
  280.7 1.3 copy-start.7
  280.7 1.7 copy-start.13
  280.7 3.0 copy-start.15
  285.9 39.4 %copy-start.8 = (f32[1,256,8,128]{1,3,2,0:T(8,128)S(1)}, f32[1,256,8,128]{1,3,2,0:T(8,128)}, u32[]{:S(2)}) copy-start(f32[1,256,8,128]{1,3,2,0:T(8,128)} %convolution_bitcast_fusion.5) | copy-start | bytes 3145732
  325.3 3.3 copy-start.5
  326.4 218.8 %copy-start.1 = (bf16[1,256,3072]{2,1,0:T(8,128)(2,1)S(1)}, bf16[1,256,3072]{2,1,0:T(8,128)(2,1)}, u32[]{:S(2)}) copy-start(bf16[1,256,3072]{2,1,0:T(8,128)(2,1)} %param.15) | copy-start | bytes 4718596
Sparse Core Ops, SparseCore 0:
  11.8 106.5 all-gather.6
  121.5 71.6 all-gather.8
  195.8 76.6 all-gather.10
  275.5 39.5 reduce-scatter.2
  321.7 223.4 reduce-scatter.4
where the time goes:
time: 555 us; the launch traced here: 552 us
  waiting for transfers between devices  320 us (58%)
  other arithmetic  76 us (14%)
  blocking collectives  63.6 us (11%)
  matrix products  43.5 us (8%)
  local copies, waits for them, and re-layouts  31.6 us (6%)
  between operations  14.7 us (3%)
    reduce_scatter x1, waiting for transfers between devices, shards(): lax.psum_scatter(jnp.einsum('thd,to->dho', attended_row_list, cotangent,...  214 us
    all_gather x1, waiting for transfers between devices, shards(): panel = lax.all_gather(w_out, ('ctx', 'dp'), axis=0, tiled=True)  105 us
    select_n x64, other arithmetic, lap(): return jax.tree.map(lambda a, b: jnp.where(reached, a, b), new, before)  75.7 us
    unnamed x1, blocking collectives  63.6 us
    dot_general x1, matrix products, shards(): jnp.einsum('thd,dho->to', attended_row_list, panel, preferred_element_typ...  17.9 us
    transpose x1, local copies, waits for them, and re-layouts, shards(): jnp.einsum('thd,to->dho', attended_row_list, cotangent, preferred_element...  16.7 us
    unnamed x44, local copies, waits for them, and re-layouts  12.5 us
  transfers between devices with their start and end apart: 5, of which 2 were waited for; matrix products, arithmetic and copies ran while one was open for 26% of the time, Pallas kernels for 0%

commit v1 on v0

--- a/solution.py
+++ b/solution.py
@@ -89,7 +89,10 @@
     )
     attended = (intra + inter * decay_multiplier).astype(jnp.bfloat16)
     attended_row_list = attended.reshape(length_here, groups, DH)
-    panel = lax.all_gather(w_out, ("ctx", "dp"), axis=0, tiled=True)
+    panel = jnp.concatenate(
+        lax.all_to_all(jnp.stack([w_out] * lax.axis_size(("ctx", "dp"))), ("ctx", "dp"), 0, 0),
+        axis=0,
+    )
     partial_out = jnp.einsum(
         "thd,dho->to", attended_row_list, panel, preferred_element_type=jnp.float32
     )

time: 555 us -> 596 us (1.074)
  local copies, waits for them, and re-layouts: 31.6 us -> 53.7 us
  blocking collectives: 63.6 us -> 83.2 us
  starting transfers between devices: 0.42 us -> 16.1 us
  matrix products: 43.5 us -> 33 us
  waiting for transfers between devices: 320 us -> 313 us
    all_to_all x0 -> x1, waiting for transfers between devices: none -> 120 us  [shards(): lax.all_to_all(jnp.stack([w_out] * lax.axis_size(('ctx', 'dp'))), ('ctx',...]
    all_gather x1 -> x0, waiting for transfers between devices: 105 us -> none  [shards(): panel = lax.all_gather(w_out, ('ctx', 'dp'), axis=0, tiled=True)]
    reduce_scatter x1, waiting for transfers between devices: 214 us -> 193 us  [shards(): lax.psum_scatter(jnp.einsum('thd,to->dho', attended_row_list, cotangent,...]
    unnamed x1, blocking collectives: 63.6 us -> 83.2 us
    all_to_all x0 -> x1, starting transfers between devices: none -> 15.8 us  [shards(): lax.all_to_all(jnp.stack([w_out] * lax.axis_size(('ctx', 'dp'))), ('ctx',...]
    reshape x1 -> x2, local copies, waits for them, and re-layouts: 1.25 us -> 14.9 us  [the longest x1 13.6 us: shards(): jnp.concatenate(lax.all_to_all(jnp.stack([w_out] * lax.axis_size(('ctx',...]
    dot_general x1, matrix products: 17.9 us -> 5.71 us  [shards(): jnp.einsum('thd,dho->to', attended_row_list, panel, preferred_element_typ...]
    all_to_all x0 -> x1, local copies, waits for them, and re-layouts: none -> 6.91 us  [shards(): lax.all_to_all(jnp.stack([w_out] * lax.axis_size(('ctx', 'dp'))), ('ctx',...]
where the time goes in v1:
time: 596 us; the launch traced here: 592 us
  waiting for transfers between devices  313 us (53%)
  blocking collectives  83.2 us (14%)
  other arithmetic  76.1 us (13%)
  local copies, waits for them, and re-layouts  53.7 us (9%)
  matrix products  33 us (6%)
  starting transfers between devices  16.1 us (3%)
  between operations  14.7 us (2%)
    reduce_scatter x1, waiting for transfers between devices, shards(): lax.psum_scatter(jnp.einsum('thd,to->dho', attended_row_list, cotangent,...  193 us
    all_to_all x1, waiting for transfers between devices, shards(): lax.all_to_all(jnp.stack([w_out] * lax.axis_size(('ctx', 'dp'))), ('ctx',...  120 us
    unnamed x1, blocking collectives  83.2 us
    select_n x64, other arithmetic, lap(): return jax.tree.map(lambda a, b: jnp.where(reached, a, b), new, before)  75.7 us
    transpose x1, local copies, waits for them, and re-layouts, shards(): jnp.einsum('thd,to->dho', attended_row_list, cotangent, preferred_element...  16.7 us
    all_to_all x1, starting transfers between devices, shards(): lax.all_to_all(jnp.stack([w_out] * lax.axis_size(('ctx', 'dp'))), ('ctx',...  15.8 us
    reshape x1, local copies, waits for them, and re-layouts, shards(): jnp.concatenate(lax.all_to_all(jnp.stack([w_out] * lax.axis_size(('ctx',...  13.6 us
  transfers between devices with their start and end apart: 5, of which 2 were waited for; matrix products, arithmetic and copies ran while one was open for 26% of the time, Pallas kernels for 0%

profile of v1, /device:TPU:1, one launch (start us, length us, event | category | flops | bytes accessed | tf_op | source)
XLA Modules:
  0.0 591.9 jit_solution(16406023710529506311)
XLA Ops:
  10.0 1.3 copy.94
  12.6 4.4 stack.2
  17.0 15.8 %all-to-all-start = ((bf16[64,2,8,3072]{3,1,2,0:T(2,128)(2,1)}), bf16[64,2,8,3072]{3,1,2,0:T(2,128)(2,1)}, u32[]{:S(2)}, u32[]{:S(2)}) async-start(bf16[64,2,8,3072]{3,1,2,0:T(2,128)(2,1)} %stack.2), calls=%async_computation | async-start | bytes 12582912 | tf_op jit(solution)/shard_map/all_to_all | solution.py:93
  32.8 1.2 copy.92
  34.1 120.0 %all-to-all-done = bf16[64,2,8,3072]{3,1,2,0:T(2,128)(2,1)} async-done(((bf16[64,2,8,3072]{3,1,2,0:T(2,128)(2,1)}), bf16[64,2,8,3072]{3,1,2,0:T(2,128)(2,1)}, u32[]{:S(2)}, u32[]{:S(2)}) %all-to-all-start) | async-done | bytes 6291488 | tf_op jit(solution)/shard_map/all_to_all | solution.py:93
  154.1 6.9 %copy.68 = bf16[64,2,8,3072]{3,1,0,2:T(2,128)(2,1)} copy(bf16[64,2,8,3072]{3,1,2,0:T(2,128)(2,1)} %all-to-all-done) | data formatting | bytes 12582912 | tf_op jit(solution)/shard_map/all_to_all | solution.py:93
  161.0 13.6 %reshape.169 = bf16[128,8,3072]{2,0,1:T(8,128)(2,1)} reshape(bf16[64,2,8,3072]{3,1,0,2:T(2,128)(2,1)} %copy.68) | data formatting | bytes 12582912 | tf_op jit(solution)/shard_map/reshape | solution.py:92
  174.6 4.6 fusion.18
  182.0 83.2 %all-reduce = f32[256]{0:T(256)S(1)} all-reduce(f32[256]{0:T(256)S(1)} %dynamic-update-slice), channel_id=2, replica_groups=mesh['ctx'=32,'head'=4,'dp'=2] {'ctx'}, use_global_device_ids=true, to_apply=%add | all-reduce | flops 256 | bytes 2048
  265.3 1.8 multiply_convert_fusion.1
  268.1 1.4 convolution_bitcast_fusion.9
  269.5 39.1 %while.30 = (s32[]{:T(128)}, f32[8,128,128]{2,1,0:T(8,128)S(1)}, s32[]{:T(128)}, f32[32,8]{1,0:T(8,128)S(1)}, f32[32,8,128,128]{3,2,1,0:T(8,128)}, /*index=5*/s32[]{:T(128)}, s32[]{:T(128)}) while((s32[]{:T(128)}, f32[8,128,128]{2,1,0:T(8,128)S(1)}, s32[]{:T(128)}, f32[32,8]{1,0:T(8,128)S(1)}, f32[32,8,128,128]{3,2,1,0:T(8,128)}, ...), condition=%wide.region_1.2_spmd.clone, body=%wide.region_0.1_spmd.clone.sunk | while | flops 524292 | bytes 1573073 | solution.py:25
  273.2 1.3 fusion.55
  308.6 1.7 fusion.21
  310.3 5.7 fusion.2
  316.3 6.3 %convolution_bitcast_fusion = f32[128,8,3072]{2,0,1:T(8,128)} fusion(bf16[256,8,128]{2,0,1:T(8,128)(2,1)S(1)} %fusion.21, bf16[1,256,3072]{2,1,0:T(8,128)(2,1)S(1)} %copy-done), kind=kOutput, calls=%fused_computation.6 | convolution fusion | flops 1610612736 | bytes 14680064 | tf_op jit(solution)/shard_map/thd,to->dho/dot_general | solution.py:108
  322.6 16.7 %copy.81 = f32[128,8,3072]{2,1,0:T(8,128)} copy(f32[128,8,3072]{2,0,1:T(8,128)} %convolution_bitcast_fusion) | data formatting | bytes 25165824 | tf_op jit(solution)/shard_map/thd,to->dho/transpose | solution.py:108
  340.3 2.5 convolution_bitcast_fusion.7
  343.6 1.4 convolution_bitcast_fusion.6
  347.2 39.5 %while.31 = (s32[]{:T(128)}, f32[8,128,128]{2,1,0:T(8,128)S(1)}, s32[]{:T(128)}, f32[32,8,128,128]{3,2,1,0:T(8,128)}, f32[32,8]{1,0:T(8,128)S(1)}, /*index=5*/s32[]{:T(128)}, s32[]{:T(128)}, s32[]{:T(128)}, s32[]{:T(128)}) while((s32[]{:T(128)}, f32[8,128,128]{2,1,0:T(8,128)S(1)}, s32[]{:T(128)}, f32[32,8,128,128]{3,2,1,0:T(8,128)}, ...), condition=%wide.region_4.5_spmd.clone, body=%wide.region_3.4_spmd.clone.sunk | while | flops 524296 | bytes 1573135 | solution.py:25
  347.2 1.3 fusion.56
  371.8 1.2 fusion.56
  374.3 1.2 fusion.56
  375.5 1.2 fusion.56
  378.0 1.2 fusion.56
  380.5 1.2 fusion.56
  381.8 1.2 fusion.56
  383.0 1.2 fusion.56
  385.5 1.2 fusion.56
  387.9 2.2 copy.84
  390.0 1.6 fusion.16
  392.6 192.8 %reduce-scatter.5.cloned.1.call-done = f32[2,8,3072]{2,1,0:T(8,128)} async-done(((f32[128,8,3072]{2,1,0:T(8,128)}), f32[2,8,3072]{2,1,0:T(8,128)}) %reduce-scatter.5.cloned.1.call-update) | async-done | bytes 196624 | tf_op jit(solution)/shard_map/reduce_scatter | solution.py:107
  (181 shorter events, 77.7 us)
Async XLA Ops:
  7.2 167.5 %copy-start = (bf16[1,256,3072]{2,1,0:T(8,128)(2,1)S(1)}, bf16[1,256,3072]{2,1,0:T(8,128)(2,1)}, u32[]{:S(2)}) copy-start(bf16[1,256,3072]{2,1,0:T(8,128)(2,1)} %param.15) | copy-start | bytes 4718596
  7.2 262.3 %all-gather.6.cloned.1.call-start = ((), (), s32[]{:S(2)}) async-start(), calls=%async_computation.5 | async-start | bytes 17301504 | tf_op jit(solution)/shard_map/all_gather | solution.py:12
  9.7 2.8 copy-start.7
  9.7 2.8 copy-start.13
  10.0 7.0 %copy-start.11 = (bf16[256,8,128]{0,2,1:T(8,128)(2,1)}, bf16[256,8,128]{0,2,1:T(8,128)(2,1)S(1)}, u32[]{:S(2)}) copy-start(bf16[256,8,128]{0,2,1:T(8,128)(2,1)S(1)} %copy.62) | copy-start | bytes 1572868
  11.4 255.8 %copy-start.2 = (bf16[32,8,8,128]{3,2,1,0:T(8,128)(2,1)}, bf16[32,8,8,128]{3,2,1,0:T(8,128)(2,1)S(1)}, u32[]{:S(2)}) copy-start(bf16[32,8,8,128]{3,2,1,0:T(8,128)(2,1)S(1)} %copy.94) | copy-start | bytes 1572868
  17.0 137.1 %all-to-all-start = ((bf16[64,2,8,3072]{3,1,2,0:T(2,128)(2,1)}), bf16[64,2,8,3072]{3,1,2,0:T(2,128)(2,1)}, u32[]{:S(2)}, u32[]{:S(2)}) async-start(bf16[64,2,8,3072]{3,1,2,0:T(2,128)(2,1)} %stack.2), calls=%async_computation | async-start | bytes 12582912 | tf_op jit(solution)/shard_map/all_to_all | solution.py:93
  32.8 314.4 %all-gather.8.cloned.1.call-start = ((), (), s32[]{:S(2)}) async-start(), calls=%async_computation.6 | async-start | bytes 17301504 | tf_op jit(solution)/shard_map/all_gather | solution.py:12
  179.2 1.2 copy-start.5
  179.2 1.2 copy-start.14
  180.4 212.3 %reduce-scatter.3.cloned.1.call-start = ((), (), s32[]{:S(2)}) async-start(), calls=%async_computation.3 | async-start | bytes 1966080 | tf_op jit(solution)/shard_map/reduce_scatter | solution.py:99
  267.1 1.0 copy-start.10
  316.1 269.3 %reduce-scatter.5.cloned.1.call-start = ((), (), s32[]{:S(2)}) async-start(), calls=%async_computation.4 | async-start | bytes 12779520 | tf_op jit(solution)/shard_map/reduce_scatter | solution.py:107
  339.3 1.0 copy-start.6
  339.3 3.5 copy-start.3
  343.6 1.4 copy-start.12
  347.2 39.5 %copy-start.8 = (bf16[32,8,8,128]{3,2,1,0:T(8,128)(2,1)S(1)}, bf16[32,8,8,128]{3,2,1,0:T(8,128)(2,1)}, u32[]{:S(2)}) copy-start(bf16[32,8,8,128]{3,2,1,0:T(8,128)(2,1)} %copy-done.7) | copy-start | bytes 1572868
  347.2 39.5 %copy-start.9 = (f32[1,256,8,128]{1,3,2,0:T(8,128)S(1)}, f32[1,256,8,128]{1,3,2,0:T(8,128)}, u32[]{:S(2)}) copy-start(f32[1,256,8,128]{1,3,2,0:T(8,128)} %convolution_bitcast_fusion.7) | copy-start | bytes 3145732
  386.7 3.4 copy-start.4
  387.9 197.5 %copy-start.1 = (bf16[1,256,3072]{2,1,0:T(8,128)(2,1)S(1)}, bf16[1,256,3072]{2,1,0:T(8,128)(2,1)}, u32[]{:S(2)}) copy-start(bf16[1,256,3072]{2,1,0:T(8,128)(2,1)} %param.15) | copy-start | bytes 4718596
Sparse Core Ops, SparseCore 0:
  12.6 146.2 all-gather.5
  180.5 97.6 all-gather.7
  316.2 38.9 reduce-scatter.2
  361.9 223.4 reduce-scatter.4
